TPU v7x, 32 devices: a whole 2x2x4 slice. The times are simulated.
32 devices in a mesh: groups: 2 (over x), row: 8 (over z, y), col: 2 (over core).
Axes of the slice: x: 2, y: 2, z: 4, core: 2. Of those that a mesh axis runs over, the one named last changes fastest.
Arguments:
- pair_repr: bfloat16 [64, 32, 128], P(('groups', 'row'), 'col'), parts along dimension 0, may hold values from -6 to 6
- in_gain: float32 [128], replicated, may hold values from 0.5 to 1.5
- in_bias: float32 [128], replicated, may hold values from -0.5 to 0.5
- left_gate_w: bfloat16 [128, 128], replicated, may hold values from -0.5 to 0.5
- left_w: bfloat16 [128, 128], replicated, may hold values from -0.5 to 0.5
- right_gate_w: bfloat16 [128, 128], replicated, may hold values from -0.5 to 0.5
- right_w: bfloat16 [128, 128], replicated, may hold values from -0.5 to 0.5
- out_gate_w: bfloat16 [128, 128], replicated, may hold values from -0.5 to 0.5
- mid_gain: float32 [128], replicated, may hold values from 0.5 to 1.5
- mid_bias: float32 [128], replicated, may hold values from -0.5 to 0.5
- out_w: bfloat16 [128, 128], replicated, may hold values from -0.5 to 0.5
Outputs:
- update: bfloat16 [64, 32, 128], P(('groups', 'row'), 'col'), parts along dimension 0
There are 2 independent parts, one for each index of `groups`. A program takes and returns all parts, laid end to end along the dimension named above; an argument that names none is the same for every part. Nothing has to cross between parts.
All inputs are finite; a program needn't handle non-finite values.
Results may differ from a plain program's by a relative error of at most 0.015.
Values may be sent and summed in bfloat16 or wider, within the bound.
A program may use at most 64 MiB of HBM per device.

v0:
```python
import jax
import jax.numpy as jnp
from jax import lax
from jax.sharding import PartitionSpec as P


def layer_norm(values, norm_gain, norm_bias):
    average = jnp.mean(values, axis=-1, keepdims=True)
    centred = values - average
    variance = jnp.mean(centred * centred, axis=-1, keepdims=True)
    return centred / jnp.sqrt(variance + 1e-05) * norm_gain + norm_bias


def on_device(
    pair_repr,
    in_gain,
    in_bias,
    left_gate_w,
    left_w,
    right_gate_w,
    right_w,
    out_gate_w,
    mid_gain,
    mid_bias,
    out_w,
):
    row_count, col_count, channels = pair_repr.shape
    hidden = left_w.shape[1]
    normed = layer_norm(pair_repr.astype(jnp.float32), in_gain, in_bias).astype(jnp.bfloat16)
    flattened = normed.reshape(row_count * col_count, channels)
    left_side = (
        (
            jax.nn.sigmoid(jnp.dot(flattened, left_gate_w, preferred_element_type=jnp.float32))
            * jnp.dot(flattened, left_w, preferred_element_type=jnp.float32)
        )
        .astype(jnp.bfloat16)
        .reshape(row_count, col_count, hidden)
    )
    right_side = (
        (
            jax.nn.sigmoid(jnp.dot(flattened, right_gate_w, preferred_element_type=jnp.float32))
            * jnp.dot(flattened, right_w, preferred_element_type=jnp.float32)
        )
        .astype(jnp.bfloat16)
        .reshape(row_count, col_count, hidden)
    )
    gating = jax.nn.sigmoid(jnp.dot(flattened, out_gate_w, preferred_element_type=jnp.float32))
    left_full = lax.all_gather(left_side, "col", axis=1, tiled=True)
    right_all = lax.all_gather(right_side, "row", axis=0, tiled=True)
    right_mine = lax.all_to_all(right_all, "col", split_axis=0, concat_axis=1, tiled=True)
    triangle = jnp.einsum("ikh,jkh->ijh", left_full, right_mine, preferred_element_type=jnp.float32)
    middle = (
        layer_norm(triangle, mid_gain, mid_bias)
        .astype(jnp.bfloat16)
        .reshape(row_count * col_count, hidden)
    )
    result = gating * jnp.dot(middle, out_w, preferred_element_type=jnp.float32)
    return result.astype(jnp.bfloat16).reshape(row_count, col_count, channels)


def solution(mesh):
    in_specs = (P(("groups", "row"), "col", None), P(), P(), P(), P(), P(), P(), P(), P(), P(), P())
    out_specs = P(("groups", "row"), "col", None)
    return jax.shard_map(
        on_device, mesh=mesh, in_specs=in_specs, out_specs=out_specs, check_vma=False
    )
```

profile of v0, /device:TPU:0, one launch (start us, length us, event | category | flops | bytes accessed | tf_op | source)
XLA Modules:
  0.0 45.9 jit_solution(8318891046903231604)
XLA Ops:
  0.0 0.0 copy-start
  0.0 0.9 %convert_reduce_fusion = f32[4,16]{1,0:T(4,128)S(1)} fusion(bf16[4,16,128]{2,1,0:T(8,128)(2,1)} %param.11), kind=kLoop, calls=%fused_computation.19 | loop fusion | flops 16320 | bytes 16640 | tf_op jit(solution)/shard_map/reduce_sum | solution.py:8
  0.9 0.0 copy-done.1
  0.9 0.2 fusion.14
  1.1 0.6 %copy-done.5 = f32[128]{0:T(128)S(1)} copy-done((f32[128]{0:T(128)S(1)}, f32[128]{0:T(128)}, u32[]{:S(2)}) %copy-start.5) | copy-done | bytes 536
  1.7 0.0 copy-done.6
  1.7 0.1 fusion.17
  1.8 0.0 copy-start.2
  1.8 0.1 fusion.5
  2.0 0.6 %copy-done.2 = bf16[128,128]{1,0:T(8,128)(2,1)S(1)} copy-done((bf16[128,128]{1,0:T(8,128)(2,1)S(1)}, bf16[128,128]{1,0:T(8,128)(2,1)}, u32[]{:S(2)}) %copy-start.2) | copy-done | bytes 32792
  2.6 0.1 fusion.9
  2.7 32.3 %all_gather.6 = bf16[32,16,128]{2,1,0:T(8,128)(2,1)S(1)} all-gather(bf16[4,16,128]{2,1,0:T(8,128)(2,1)S(1)} %bitcast.37), channel_id=1, replica_groups=mesh['groups'=2,'row'=8,'col'=2] {'row'}, dimensions={0}, use_global_device_ids=true | all-gather | bytes 147456 | tf_op jit(solution)/shard_map/all_gather | solution.py:49
  35.0 3.8 %all_to_all.18 = bf16[32,16,128]{2,1,0:T(8,128)(2,1)S(1)} all-to-all(bf16[32,16,128]{2,1,0:T(8,128)(2,1)S(1)} %all_gather.6), channel_id=1, replica_groups=mesh['groups'=2,'row'=8,'col'=2] {'col'}, dimensions={0} | all-to-all | bytes 262144 | tf_op jit(solution)/shard_map/all_to_all | solution.py:50
  38.9 0.0 copy-start.9
  38.9 0.4 copy.28
  39.3 0.3 copy-done.9
  39.6 0.1 fusion.2
  39.8 0.6 %copy-done.3 = bf16[128,128]{1,0:T(8,128)(2,1)S(1)} copy-done((bf16[128,128]{1,0:T(8,128)(2,1)S(1)}, bf16[128,128]{1,0:T(8,128)(2,1)}, u32[]{:S(2)}) %copy-start.3) | copy-done | bytes 32792
  40.4 0.1 fusion.10
  40.5 1.8 %all_gather.7 = bf16[4,32,128]{2,0,1:T(4,128)(2,1)S(1)} all-gather(bf16[4,16,128]{2,0,1:T(4,128)(2,1)S(1)} %copy.27), channel_id=1, replica_groups=mesh['groups'=2,'row'=8,'col'=2] {'col'}, dimensions={1}, use_global_device_ids=true | all-gather | bytes 49152 | tf_op jit(solution)/shard_map/all_gather | solution.py:48
  42.4 0.1 copy.29
  42.5 0.4 fusion.18
  42.9 0.1 copy.30
  43.0 0.1 bitcast_reduce_fusion
  43.1 0.2 multiply_reduce_fusion
  43.3 0.5 %copy-done.10 = bf16[128,128]{1,0:T(8,128)(2,1)S(1)} copy-done((bf16[128,128]{1,0:T(8,128)(2,1)S(1)}, bf16[128,128]{1,0:T(8,128)(2,1)}, u32[]{:S(2)}) %copy-start.10) | copy-done | bytes 32792
  43.8 0.1 fusion.8
  43.9 0.5 %copy-done.7 = f32[128]{0:T(128)S(1)} copy-done((f32[128]{0:T(128)S(1)}, f32[128]{0:T(128)}, u32[]{:S(2)}) %copy-start.7) | copy-done | bytes 536
  44.4 0.0 copy-done.8
  44.4 0.1 add_convert_fusion
  44.5 0.7 %copy-done.4 = bf16[128,128]{1,0:T(8,128)(2,1)S(1)} copy-done((bf16[128,128]{1,0:T(8,128)(2,1)S(1)}, bf16[128,128]{1,0:T(8,128)(2,1)}, u32[]{:S(2)}) %copy-start.4) | copy-done | bytes 32792
  45.2 0.7 %fusion.11 = bf16[64,128]{1,0:T(8,128)(2,1)} fusion(f32[64,128]{1,0:T(8,128)S(1)} %fusion.8, bf16[64,128]{1,0:T(8,128)(2,1)S(1)} %bitcast.38, bf16[128,128]{1,0:T(8,128)(2,1)S(1)} %copy-done.4), kind=kOutput, calls=%fused_computation.17 | convolution fusion | flops 2113536 | bytes 98304 | tf_op jit(solution)/shard_map/dot_general | solution.py:57
  (15 shorter events, 0.1 us)
Async XLA Ops:
  0.0 1.8 %copy-start = (bf16[128,128]{1,0:T(8,128)(2,1)S(1)}, bf16[128,128]{1,0:T(8,128)(2,1)}, u32[]{:S(2)}) copy-start(bf16[128,128]{1,0:T(8,128)(2,1)} %param.16) | copy-start | bytes 98308
  0.0 0.9 %copy-start.1 = (bf16[4,16,128]{2,1,0:T(8,128)(2,1)S(1)}, bf16[4,16,128]{2,1,0:T(8,128)(2,1)}, u32[]{:S(2)}) copy-start(bf16[4,16,128]{2,1,0:T(8,128)(2,1)} %param.11) | copy-start | bytes 49156
  1.0 0.7 %copy-start.5 = (f32[128]{0:T(128)S(1)}, f32[128]{0:T(128)}, u32[]{:S(2)}) copy-start(f32[128]{0:T(128)} %param.13) | copy-start | bytes 1540
  1.1 0.7 %copy-start.6 = (f32[128]{0:T(128)S(1)}, f32[128]{0:T(128)}, u32[]{:S(2)}) copy-start(f32[128]{0:T(128)} %param.12) | copy-start | bytes 1540
  1.8 0.8 %copy-start.2 = (bf16[128,128]{1,0:T(8,128)(2,1)S(1)}, bf16[128,128]{1,0:T(8,128)(2,1)}, u32[]{:S(2)}) copy-start(bf16[128,128]{1,0:T(8,128)(2,1)} %param.17) | copy-start | bytes 98308
  38.9 0.8 %copy-start.9 = (bf16[128,128]{1,0:T(8,128)(2,1)S(1)}, bf16[128,128]{1,0:T(8,128)(2,1)}, u32[]{:S(2)}) copy-start(bf16[128,128]{1,0:T(8,128)(2,1)} %param.14) | copy-start | bytes 98308
  39.6 0.8 %copy-start.3 = (bf16[128,128]{1,0:T(8,128)(2,1)S(1)}, bf16[128,128]{1,0:T(8,128)(2,1)}, u32[]{:S(2)}) copy-start(bf16[128,128]{1,0:T(8,128)(2,1)} %param.15) | copy-start | bytes 98308
  43.0 0.8 %copy-start.10 = (bf16[128,128]{1,0:T(8,128)(2,1)S(1)}, bf16[128,128]{1,0:T(8,128)(2,1)}, u32[]{:S(2)}) copy-start(bf16[128,128]{1,0:T(8,128)(2,1)} %param.18) | copy-start | bytes 98308
  43.8 0.7 %copy-start.7 = (f32[128]{0:T(128)S(1)}, f32[128]{0:T(128)}, u32[]{:S(2)}) copy-start(f32[128]{0:T(128)} %param.20) | copy-start | bytes 1540
  43.8 0.7 %copy-start.8 = (f32[128]{0:T(128)S(1)}, f32[128]{0:T(128)}, u32[]{:S(2)}) copy-start(f32[128]{0:T(128)} %param.19) | copy-start | bytes 1540
  44.4 0.8 %copy-start.4 = (bf16[128,128]{1,0:T(8,128)(2,1)S(1)}, bf16[128,128]{1,0:T(8,128)(2,1)}, u32[]{:S(2)}) copy-start(bf16[128,128]{1,0:T(8,128)(2,1)} %param.21) | copy-start | bytes 98308
where the time goes:
time: 46.5 us; the launch traced here: 45.9 us
  blocking collectives  38 us (82%)
  local copies, waits for them, and re-layouts  4.56 us (10%)
  matrix products  1.79 us (4%)
  other arithmetic  1.48 us (3%)
    all_gather x1, blocking collectives, on_device(): right_all = lax.all_gather(right_side, 'row', axis=0, tiled=True)  32.3 us
    unnamed x22, local copies, waits for them, and re-layouts  3.86 us
    all_to_all x1, blocking collectives, on_device(): lax.all_to_all(right_all, 'col', split_axis=0, concat_axis=1, tiled=True)  3.83 us
    all_gather x1, blocking collectives, on_device(): left_full = lax.all_gather(left_side, 'col', axis=1, tiled=True)  1.83 us
    reduce_sum x2, other arithmetic, layer_norm(): average = jnp.mean(values, axis=-1, keepdims=True)  0.96 us

commit v1 on v0

--- a/solution.py
+++ b/solution.py
@@ -46,7 +46,12 @@
     )
     gating = jax.nn.sigmoid(jnp.dot(flattened, out_gate_w, preferred_element_type=jnp.float32))
     left_full = lax.all_gather(left_side, "col", axis=1, tiled=True)
-    right_all = lax.all_gather(right_side, "row", axis=0, tiled=True)
+    ring = [right_side]
+    for hop in range(7):
+        ring.append(lax.ppermute(ring[-1], "row", [(dev, (dev + 1) % 8) for dev in range(8)]))
+    right_all = jnp.roll(
+        jnp.concatenate(ring[::-1], axis=0), (lax.axis_index("row") + 1) * ring[0].shape[0], axis=0
+    )
     right_mine = lax.all_to_all(right_all, "col", split_axis=0, concat_axis=1, tiled=True)
     triangle = jnp.einsum("ikh,jkh->ijh", left_full, right_mine, preferred_element_type=jnp.float32)
     middle = (

time: 46.5 us -> 56.2 us (1.21)
  waiting for transfers between devices: 0 us -> 40.9 us
  blocking collectives: 38 us -> 5.67 us
  starting transfers between devices: 0 us -> 2.99 us
  local copies, waits for them, and re-layouts: 4.56 us -> 2.8 us
    ppermute x0 -> x7, waiting for transfers between devices: none -> 40.9 us  [on_device(): lax.ppermute(ring[-1], 'row', [(dev, (dev + 1) % 8) for dev in range(8)])]
    all_gather x1 -> x0, blocking collectives: 32.3 us -> none  [on_device(): right_all = lax.all_gather(right_side, 'row', axis=0, tiled=True)]
    ppermute x0 -> x7, starting transfers between devices: none -> 2.99 us  [on_device(): lax.ppermute(ring[-1], 'row', [(dev, (dev + 1) % 8) for dev in range(8)])]
    unnamed x22 -> x37, local copies, waits for them, and re-layouts: 3.86 us -> 2.07 us
  transfers between devices with their start and end apart: 0 -> 7, of which waited for: 0 -> 7; matrix products, arithmetic and copies ran while one was open for 0% -> 1% of each run, Pallas kernels for 0% -> 0%
where the time goes in v1:
time: 56.2 us; the launch traced here: 55.9 us
  waiting for transfers between devices  40.9 us (73%)
  blocking collectives  5.67 us (10%)
  starting transfers between devices  2.99 us (5%)
  local copies, waits for them, and re-layouts  2.8 us (5%)
  matrix products  1.8 us (3%)
  other arithmetic  1.49 us (3%)
    ppermute x7, waiting for transfers between devices, on_device(): lax.ppermute(ring[-1], 'row', [(dev, (dev + 1) % 8) for dev in range(8)])  40.9 us
    all_to_all x1, blocking collectives, on_device(): lax.all_to_all(right_all, 'col', split_axis=0, concat_axis=1, tiled=True)  3.84 us
    ppermute x7, starting transfers between devices, on_device(): lax.ppermute(ring[-1], 'row', [(dev, (dev + 1) % 8) for dev in range(8)])  2.99 us
    unnamed x37, local copies, waits for them, and re-layouts  2.07 us
    all_gather x1, blocking collectives, on_device(): left_full = lax.all_gather(left_side, 'col', axis=1, tiled=True)  1.83 us
  transfers between devices with their start and end apart: 7, of which 7 were waited for; matrix products, arithmetic and copies ran while one was open for 1% of the time, Pallas kernels for 0%

profile of v1, /device:TPU:0, one launch (start us, length us, event | category | flops | bytes accessed | tf_op | source)
XLA Modules:
  0.0 55.9 jit_solution(16911057987291468324)
XLA Ops:
  0.0 0.9 %convert_reduce_fusion = f32[4,16]{1,0:T(4,128)S(1)} fusion(bf16[4,16,128]{2,1,0:T(8,128)(2,1)} %param.11), kind=kLoop, calls=%fused_computation.19 | loop fusion | flops 16320 | bytes 16640 | tf_op jit(solution)/shard_map/reduce_sum | solution.py:8
  0.9 0.2 fusion.14
  1.1 0.6 %copy-done.5 = f32[128]{0:T(128)S(1)} copy-done((f32[128]{0:T(128)S(1)}, f32[128]{0:T(128)}, u32[]{:S(2)}) %copy-start.5) | copy-done | bytes 536
  1.7 0.0 copy-done.6
  1.7 0.1 fusion.17
  1.8 0.1 fusion.5
  2.0 0.6 %copy-done.2 = bf16[128,128]{1,0:T(8,128)(2,1)S(1)} copy-done((bf16[128,128]{1,0:T(8,128)(2,1)S(1)}, bf16[128,128]{1,0:T(8,128)(2,1)}, u32[]{:S(2)}) %copy-start.2) | copy-done | bytes 32792
  2.6 0.1 fusion.9
  2.7 3.0 %collective-permute-start = (bf16[4,16,128]{2,1,0:T(8,128)(2,1)S(1)}, bf16[4,16,128]{2,1,0:T(8,128)(2,1)S(1)}, u32[]{:S(2)}, u32[]{:S(2)}) collective-permute-start(bf16[4,16,128]{2,1,0:T(8,128)(2,1)S(1)} %bitcast.32), channel_id=1, source_target_pairs={{0,2},{2,4},{4,6},{6,8},{8,10},{10,12},{12,14},{14,0},{1,3},{3,5},... | collective-permute-start | bytes 49160 | tf_op jit(solution)/shard_map/ppermute | solution.py:51
  5.7 4.8 %collective-permute-done = bf16[4,16,128]{2,1,0:T(8,128)(2,1)S(1)} collective-permute-done((bf16[4,16,128]{2,1,0:T(8,128)(2,1)S(1)}, bf16[4,16,128]{2,1,0:T(8,128)(2,1)S(1)}, u32[]{:S(2)}, u32[]{:S(2)}) %collective-permute-start) | collective-permute-done | bytes 16416 | tf_op jit(solution)/shard_map/ppermute | solution.py:51
  10.5 6.4 %collective-permute-done.1 = bf16[4,16,128]{2,1,0:T(8,128)(2,1)S(1)} collective-permute-done((bf16[4,16,128]{2,1,0:T(8,128)(2,1)S(1)}, bf16[4,16,128]{2,1,0:T(8,128)(2,1)S(1)}, u32[]{:S(2)}, u32[]{:S(2)}) %collective-permute-start.1) | collective-permute-done | bytes 16416 | tf_op jit(solution)/shard_map/ppermute | solution.py:51
  16.9 6.4 %collective-permute-done.2 = bf16[4,16,128]{2,1,0:T(8,128)(2,1)S(1)} collective-permute-done((bf16[4,16,128]{2,1,0:T(8,128)(2,1)S(1)}, bf16[4,16,128]{2,1,0:T(8,128)(2,1)S(1)}, u32[]{:S(2)}, u32[]{:S(2)}) %collective-permute-start.2) | collective-permute-done | bytes 16416 | tf_op jit(solution)/shard_map/ppermute | solution.py:51
  23.3 6.4 %collective-permute-done.3 = bf16[4,16,128]{2,1,0:T(8,128)(2,1)S(1)} collective-permute-done((bf16[4,16,128]{2,1,0:T(8,128)(2,1)S(1)}, bf16[4,16,128]{2,1,0:T(8,128)(2,1)S(1)}, u32[]{:S(2)}, u32[]{:S(2)}) %collective-permute-start.3) | collective-permute-done | bytes 16416 | tf_op jit(solution)/shard_map/ppermute | solution.py:51
  29.8 0.1 fusion.2
  29.9 6.3 %collective-permute-done.4 = bf16[4,16,128]{2,1,0:T(8,128)(2,1)S(1)} collective-permute-done((bf16[4,16,128]{2,1,0:T(8,128)(2,1)S(1)}, bf16[4,16,128]{2,1,0:T(8,128)(2,1)S(1)}, u32[]{:S(2)}, u32[]{:S(2)}) %collective-permute-start.4) | collective-permute-done | bytes 16416 | tf_op jit(solution)/shard_map/ppermute | solution.py:51
  36.2 0.1 fusion.10
  36.3 6.3 %collective-permute-done.5 = bf16[4,16,128]{2,1,0:T(8,128)(2,1)S(1)} collective-permute-done((bf16[4,16,128]{2,1,0:T(8,128)(2,1)S(1)}, bf16[4,16,128]{2,1,0:T(8,128)(2,1)S(1)}, u32[]{:S(2)}, u32[]{:S(2)}) %collective-permute-start.5) | collective-permute-done | bytes 16416 | tf_op jit(solution)/shard_map/ppermute | solution.py:51
  42.7 0.1 fusion.8
  42.8 1.8 %all_gather.3 = bf16[4,32,128]{2,0,1:T(4,128)(2,1)S(1)} all-gather(bf16[4,16,128]{2,0,1:T(4,128)(2,1)S(1)} %copy.27), channel_id=1, replica_groups=mesh['groups'=2,'row'=8,'col'=2] {'col'}, dimensions={1}, use_global_device_ids=true | all-gather | bytes 49152 | tf_op jit(solution)/shard_map/all_gather | solution.py:48
  44.7 0.1 copy.29
  44.8 4.3 %collective-permute-done.6 = bf16[4,16,128]{2,1,0:T(8,128)(2,1)S(1)} collective-permute-done((bf16[4,16,128]{2,1,0:T(8,128)(2,1)S(1)}, bf16[4,16,128]{2,1,0:T(8,128)(2,1)S(1)}, u32[]{:S(2)}, u32[]{:S(2)}) %collective-permute-start.6) | collective-permute-done | bytes 16416 | tf_op jit(solution)/shard_map/ppermute | solution.py:51
  49.3 3.8 %all_to_all.18 = bf16[32,16,128]{2,1,0:T(8,128)(2,1)S(1)} all-to-all(bf16[32,16,128]{2,1,0:T(8,128)(2,1)S(1)} %constant_dynamic-slice_fusion), channel_id=1, replica_groups=mesh['groups'=2,'row'=8,'col'=2] {'col'}, dimensions={0} | all-to-all | bytes 262144 | tf_op jit(solution)/shard_map/all_to_all | solution.py:55
  53.1 0.4 copy.28
  53.6 0.4 fusion.18
  53.9 0.1 copy.30
  54.1 0.1 bitcast_reduce_fusion
  54.2 0.2 multiply_reduce_fusion
  54.4 0.4 copy-done.7
  54.7 0.0 copy-done.8
  54.8 0.1 add_convert_fusion
  54.8 0.3 copy-done.4
  55.1 0.7 %fusion.11 = bf16[64,128]{1,0:T(8,128)(2,1)} fusion(f32[64,128]{1,0:T(8,128)S(1)} %fusion.8, bf16[64,128]{1,0:T(8,128)(2,1)S(1)} %bitcast.41, bf16[128,128]{1,0:T(8,128)(2,1)S(1)} %copy-done.4), kind=kOutput, calls=%fused_computation.17 | convolution fusion | flops 2113536 | bytes 98304 | tf_op jit(solution)/shard_map/dot_general | solution.py:62
  (45 shorter events, 0.3 us)
Async XLA Ops:
  0.0 1.8 %copy-start = (bf16[128,128]{1,0:T(8,128)(2,1)S(1)}, bf16[128,128]{1,0:T(8,128)(2,1)}, u32[]{:S(2)}) copy-start(bf16[128,128]{1,0:T(8,128)(2,1)} %param.16) | copy-start | bytes 98308
  0.0 0.9 %copy-start.1 = (bf16[4,16,128]{2,1,0:T(8,128)(2,1)S(1)}, bf16[4,16,128]{2,1,0:T(8,128)(2,1)}, u32[]{:S(2)}) copy-start(bf16[4,16,128]{2,1,0:T(8,128)(2,1)} %param.11) | copy-start | bytes 49156
  1.0 0.7 %copy-start.5 = (f32[128]{0:T(128)S(1)}, f32[128]{0:T(128)}, u32[]{:S(2)}) copy-start(f32[128]{0:T(128)} %param.13) | copy-start | bytes 1540
  1.1 0.7 %copy-start.6 = (f32[128]{0:T(128)S(1)}, f32[128]{0:T(128)}, u32[]{:S(2)}) copy-start(f32[128]{0:T(128)} %param.12) | copy-start | bytes 1540
  1.8 0.8 %copy-start.2 = (bf16[128,128]{1,0:T(8,128)(2,1)S(1)}, bf16[128,128]{1,0:T(8,128)(2,1)}, u32[]{:S(2)}) copy-start(bf16[128,128]{1,0:T(8,128)(2,1)} %param.17) | copy-start | bytes 98308
  2.6 27.2 %copy-start.9 = (bf16[128,128]{1,0:T(8,128)(2,1)S(1)}, bf16[128,128]{1,0:T(8,128)(2,1)}, u32[]{:S(2)}) copy-start(bf16[128,128]{1,0:T(8,128)(2,1)} %param.14) | copy-start | bytes 98308
  2.7 33.5 %copy-start.3 = (bf16[128,128]{1,0:T(8,128)(2,1)S(1)}, bf16[128,128]{1,0:T(8,128)(2,1)}, u32[]{:S(2)}) copy-start(bf16[128,128]{1,0:T(8,128)(2,1)} %param.15) | copy-start | bytes 98308
  2.7 7.7 %collective-permute-start = (bf16[4,16,128]{2,1,0:T(8,128)(2,1)S(1)}, bf16[4,16,128]{2,1,0:T(8,128)(2,1)S(1)}, u32[]{:S(2)}, u32[]{:S(2)}) collective-permute-start(bf16[4,16,128]{2,1,0:T(8,128)(2,1)S(1)} %bitcast.32), channel_id=1, source_target_pairs={{0,2},{2,4},{4,6},{6,8},{8,10},{10,12},{12,14},{14,0},{1,3},{3,5},... | collective-permute-start | bytes 49160 | tf_op jit(solution)/shard_map/ppermute | solution.py:51
  10.5 6.4 %collective-permute-start.1 = (bf16[4,16,128]{2,1,0:T(8,128)(2,1)S(1)}, bf16[4,16,128]{2,1,0:T(8,128)(2,1)S(1)}, u32[]{:S(2)}, u32[]{:S(2)}) collective-permute-start(bf16[4,16,128]{2,1,0:T(8,128)(2,1)S(1)} %collective-permute-done), channel_id=1, source_target_pairs={{0,2},{2,4},{4,6},{6,8},{8,10},{10,12},{12,14},{14,0},{1,3},{3,5},... | collective-permute-start | bytes 49160 | tf_op jit(solution)/shard_map/ppermute | solution.py:51
  16.9 6.4 %collective-permute-start.2 = (bf16[4,16,128]{2,1,0:T(8,128)(2,1)S(1)}, bf16[4,16,128]{2,1,0:T(8,128)(2,1)S(1)}, u32[]{:S(2)}, u32[]{:S(2)}) collective-permute-start(bf16[4,16,128]{2,1,0:T(8,128)(2,1)S(1)} %collective-permute-done.1), channel_id=1, source_target_pairs={{0,2},{2,4},{4,6},{6,8},{8,10},{10,12},{12,14},{14,0},{1,3},{3,5},... | collective-permute-start | bytes 49160 | tf_op jit(solution)/shard_map/ppermute | solution.py:51
  23.3 6.4 %collective-permute-start.3 = (bf16[4,16,128]{2,1,0:T(8,128)(2,1)S(1)}, bf16[4,16,128]{2,1,0:T(8,128)(2,1)S(1)}, u32[]{:S(2)}, u32[]{:S(2)}) collective-permute-start(bf16[4,16,128]{2,1,0:T(8,128)(2,1)S(1)} %collective-permute-done.2), channel_id=1, source_target_pairs={{0,2},{2,4},{4,6},{6,8},{8,10},{10,12},{12,14},{14,0},{1,3},{3,5},... | collective-permute-start | bytes 49160 | tf_op jit(solution)/shard_map/ppermute | solution.py:51
  29.8 6.4 %collective-permute-start.4 = (bf16[4,16,128]{2,1,0:T(8,128)(2,1)S(1)}, bf16[4,16,128]{2,1,0:T(8,128)(2,1)S(1)}, u32[]{:S(2)}, u32[]{:S(2)}) collective-permute-start(bf16[4,16,128]{2,1,0:T(8,128)(2,1)S(1)} %collective-permute-done.3), channel_id=1, source_target_pairs={{0,2},{2,4},{4,6},{6,8},{8,10},{10,12},{12,14},{14,0},{1,3},{3,5},... | collective-permute-start | bytes 49160 | tf_op jit(solution)/shard_map/ppermute | solution.py:51
  29.9 12.7 %copy-start.10 = (bf16[128,128]{1,0:T(8,128)(2,1)S(1)}, bf16[128,128]{1,0:T(8,128)(2,1)}, u32[]{:S(2)}) copy-start(bf16[128,128]{1,0:T(8,128)(2,1)} %param.18) | copy-start | bytes 98308
  36.2 6.4 %collective-permute-start.5 = (bf16[4,16,128]{2,1,0:T(8,128)(2,1)S(1)}, bf16[4,16,128]{2,1,0:T(8,128)(2,1)S(1)}, u32[]{:S(2)}, u32[]{:S(2)}) collective-permute-start(bf16[4,16,128]{2,1,0:T(8,128)(2,1)S(1)} %collective-permute-done.4), channel_id=1, source_target_pairs={{0,2},{2,4},{4,6},{6,8},{8,10},{10,12},{12,14},{14,0},{1,3},{3,5},... | collective-permute-start | bytes 49160 | tf_op jit(solution)/shard_map/ppermute | solution.py:51
  42.6 6.4 %collective-permute-start.6 = (bf16[4,16,128]{2,1,0:T(8,128)(2,1)S(1)}, bf16[4,16,128]{2,1,0:T(8,128)(2,1)S(1)}, u32[]{:S(2)}, u32[]{:S(2)}) collective-permute-start(bf16[4,16,128]{2,1,0:T(8,128)(2,1)S(1)} %collective-permute-done.5), channel_id=1, source_target_pairs={{0,2},{2,4},{4,6},{6,8},{8,10},{10,12},{12,14},{14,0},{1,3},{3,5},... | collective-permute-start | bytes 49160 | tf_op jit(solution)/shard_map/ppermute | solution.py:51
  54.1 0.7 %copy-start.7 = (f32[128]{0:T(128)S(1)}, f32[128]{0:T(128)}, u32[]{:S(2)}) copy-start(f32[128]{0:T(128)} %param.20) | copy-start | bytes 1540
  54.1 0.7 %copy-start.8 = (f32[128]{0:T(128)S(1)}, f32[128]{0:T(128)}, u32[]{:S(2)}) copy-start(f32[128]{0:T(128)} %param.19) | copy-start | bytes 1540
  54.3 0.8 %copy-start.4 = (bf16[128,128]{1,0:T(8,128)(2,1)S(1)}, bf16[128,128]{1,0:T(8,128)(2,1)}, u32[]{:S(2)}) copy-start(bf16[128,128]{1,0:T(8,128)(2,1)} %param.21) | copy-start | bytes 98308
